TPU v7x, 32 devices: a whole 2x2x4 slice. The times are simulated.
32 devices in a mesh: dp: 2 (over y), expert: 4 (over x, core), tensor: 4 (over z).
Axes of the slice: x: 2, y: 2, z: 4, core: 2. Of those that a mesh axis runs over, the one named last changes fastest.
Arguments:
- hidden_rows: bfloat16 [128, 7168], P(('dp', 'expert')), may hold values from -6 to 6
- expert_ids: int32 [128, 8], P(('dp', 'expert')), may hold values from 0 to 15, all different within a row; in each aligned block of 16 rows (0 to 15, 16 to 31, ...) at most 16 rows name the same one
- route_weights: float32 [128, 8], P(('dp', 'expert')), may hold values from 0.1 to 1
- w_gate: bfloat16 [16, 1024, 7168], P(('expert', 'tensor'), 'dp'), may hold values from -0.0625 to 0.0625
- w_up: bfloat16 [16, 1024, 7168], P(('expert', 'tensor'), 'dp'), may hold values from -0.0625 to 0.0625
- w_down: bfloat16 [16, 1024, 7168], P(('expert', 'tensor'), 'dp'), may hold values from -0.1875 to 0.1875
Outputs:
- moe_out: bfloat16 [128, 7168], P(('dp', 'expert'))
Inputs may be any that keep to these rules, and one draw needn't show every extreme that they name: `expert_ids`: each row names 8 different experts. Within the 16 rows of one attention group (one index of dp+expert), no expert is named by more than 16 rows, a bound that some block reaches.
All inputs are finite; a program needn't handle non-finite values.
Results may differ from a plain program's by a relative error of at most 0.0057.
Values may be sent and summed in bfloat16 or wider, within the bound.
A program may use at most 64 MiB of HBM per device.

v0:
```python
import functools

import jax
import jax.numpy as jnp
from jax import lax
from jax.experimental import pallas as pl
from jax.experimental.pallas import tpu as pltpu
from jax.sharding import PartitionSpec as P


def slot_table(route_ids, targets, capacity):
    matches = jnp.any(route_ids[:, :, None] == targets[None, None, :], axis=1)
    positions = jnp.cumsum(matches.astype(jnp.int32), axis=0) - 1
    slot_numbers = jnp.arange(capacity, dtype=jnp.int32)
    slot_hits = matches[:, :, None] & (positions[:, :, None] == slot_numbers[None, None, :])
    return jnp.transpose(slot_hits, (1, 2, 0)).astype(jnp.float32)


def route_share(route_ids, route_weights, targets):
    chosen = (route_ids[:, :, None] == targets[None, None, :]).astype(jnp.float32)
    return jnp.sum(route_weights[:, :, None] * chosen, axis=1)


def row_product(left, right):
    return lax.dot_general(
        left, right, (((1,), (1,)), ((), ())), preferred_element_type=jnp.float32
    )


def general_body(hidden_rows, expert_ids, route_weights, w_gate, w_up, w_down):
    expert_count = lax.axis_size("expert")
    tensor_count = lax.axis_size("tensor")
    lane_index = lax.axis_index("tensor")
    group_rows, feature_width = hidden_rows.shape
    chosen_count = expert_ids.shape[1]
    experts_all = expert_count * tensor_count
    capacity = min(group_rows, max(2, 2 * group_rows * chosen_count // experts_all))
    targets = jnp.arange(expert_count, dtype=jnp.int32) * tensor_count + lane_index
    own_table = slot_table(expert_ids, targets, capacity)
    all_rows, all_ids = (
        lax.all_gather(hidden_rows, "expert", axis=0, tiled=True),
        lax.all_gather(expert_ids, "expert", axis=0, tiled=True),
    )
    own_expert = lax.axis_index("expert") * tensor_count + lane_index
    own_target = jnp.reshape(own_expert, (1,))

    def group_table(route_ids):
        return slot_table(route_ids, own_target, capacity)[0]

    tables = jax.vmap(group_table)(all_ids.reshape(expert_count, group_rows, chosen_count))
    arrived = jnp.einsum(
        "gcr,grd->gcd",
        tables.astype(jnp.bfloat16),
        all_rows.reshape(expert_count, group_rows, feature_width),
        preferred_element_type=jnp.float32,
    ).astype(jnp.bfloat16)
    gate_weight = w_gate[0]
    up_weight = w_up[0]
    down_weight = w_down[0]
    block_piece = lax.all_gather(arrived, "dp", axis=0, tiled=True)
    row_count = block_piece.shape[0]
    activate_row_count = block_piece.shape[0]
    flat_rows = block_piece.reshape(activate_row_count * capacity, feature_width)
    gate_value = row_product(flat_rows, gate_weight)
    up_value = row_product(flat_rows, up_weight)
    activation = (jax.nn.silu(gate_value) * up_value).astype(jnp.bfloat16)
    down_part = jnp.dot(activation, down_weight, preferred_element_type=jnp.float32)
    partial_value = down_part.reshape(row_count, capacity, feature_width)
    summed = lax.psum_scatter(partial_value, "dp", scatter_dimension=0, tiled=True)
    expert_out = summed.astype(jnp.bfloat16)
    back_rows = lax.all_to_all(expert_out, "expert", split_axis=0, concat_axis=0, tiled=True)
    route_table = route_share(expert_ids, route_weights, targets)
    coefficient = own_table * jnp.transpose(route_table)[:, None, :]
    mixed_rows = jnp.einsum(
        "gcr,gcd->rd", coefficient, back_rows.astype(jnp.float32), precision=lax.Precision.HIGHEST
    )
    summed_rows = lax.psum(mixed_rows, "tensor")
    return summed_rows.astype(jnp.bfloat16)


def split_count(width, unit, most):
    units = width // unit
    return max(n for n in range(1, most + 1) if units % n == 0)


def split_rounds(width, count):
    units = width // 128
    edges = [-(-units * i // count) * 128 for i in range(count + 1)]
    return tuple((low, high - low) for low, high in zip(edges, edges[1:]))


def fused_kernel(
    sizes, rounds, lags,
    hid, ids, wts, wg, wu, wd, out,
    rows_all, wg_v, wu_v, wd_v, gate_acc, up_acc, act, table,
    pair_send, pair_recv, part, a_send, a_recv, b_send, b_recv, c_send, c_recv, f_send, own_total, gathered,
    ids_v, wts_v, own_sem, id_sem, w_sem, g_send, g_recv, t_send, t_recv, pa_send, pa_recv, aa_send, aa_recv,
    ba_send, ba_recv, ca_send, ca_recv, fa_send, fa_recv,
):
    dp_count, expert_count, tensor_count, chunks = sizes
    group, width = hid.shape
    chunk = width // chunks
    half = width // 2
    quarter = half // tensor_count
    block = 2 * group
    y, e, z = lax.axis_index("dp"), lax.axis_index("expert"), lax.axis_index("tensor")
    x, c = e // 2, e % 2
    xe, ce, yy = e + 2 - 4 * x, e + 1 - 2 * c, 1 - y
    cxe = ce + 2 - 4 * x

    def device(dp, expert, tensor):
        return {"dp": dp, "expert": expert, "tensor": tensor}

    def number(dp, expert):
        return dp * expert_count + expert

    def rows_of(g):
        return pl.ds(pl.multiple_of(g * group, group), group)

    def cols_of(j):
        return pl.ds(pl.multiple_of(j * chunk, chunk), chunk)

    def remote(src, dst, send, recv, target):
        return pltpu.make_async_remote_copy(
            src_ref=src, dst_ref=dst, send_sem=send, recv_sem=recv,
            device_id=target, device_id_type=pl.DeviceIdType.MESH,
        )

    plane = [
        (p, device((y + p // expert_count) % dp_count, (e + p % expert_count) % expert_count, z))
        for p in range(1, dp_count * expert_count)
    ]
    line = [
        (d, o, device(y, e if o == 0 else ce, (z + d) % tensor_count))
        for d in range(tensor_count) for o in range(2)
    ]
    barrier = pltpu.get_barrier_semaphore()
    greeted = [t for _, t in plane] + [t for d, _, t in line if d > 0]
    for target in greeted:
        pl.semaphore_signal(barrier, inc=1, device_id=target, device_id_type=pl.DeviceIdType.MESH)

    own = number(y, e)
    own_copy = pltpu.make_async_copy(hid, rows_all.at[rows_of(own), :], own_sem)
    own_copy.start()
    id_copies = [
        pltpu.make_async_copy(ids, ids_v, id_sem.at[0]), pltpu.make_async_copy(wts, wts_v, id_sem.at[1])
    ]
    for copy in id_copies:
        copy.start()

    def weight_copy(which, j):
        src, dst = ((wg, wg_v), (wu, wu_v), (wd, wd_v))[which]
        return pltpu.make_async_copy(src.at[0, :, cols_of(j)], dst.at[:, cols_of(j)], w_sem.at[which, j])

    for j in range(chunks):
        weight_copy(0, j).start()
        weight_copy(1, j).start()
    gate_acc[...] = jnp.zeros_like(gate_acc)
    up_acc[...] = jnp.zeros_like(up_acc)
    pl.semaphore_wait(barrier, len(greeted))

    to_x, to_y, to_pair = device(y, xe, z), device(yy, e, z), device(y, ce, z)
    g_x, g_y, g_d = number(y, xe), number(yy, e), number(yy, xe)
    pair_groups = (number(y, ce), number(y, cxe), number(yy, ce), number(yy, cxe))

    def piece(g, j):
        return rows_all.at[rows_of(g), cols_of(j)]

    def own_send(kind, j, target):
        return remote(hid.at[:, cols_of(j)], piece(own, j), g_send.at[kind, j], g_recv.at[kind, j], target)

    def forward(kind, g, j, target):
        return remote(piece(g, j), piece(g, j), g_send.at[kind, j], g_recv.at[kind, j], target)

    def diagonal(j):
        odd = j % 2
        target = device(y + (1 - odd) * (1 - 2 * y), e + odd * (xe - e), z)
        return forward(2, g_x + odd * (g_y - g_x), j, target)

    for j in range(chunks):
        own_send(0, j, to_x).start()
        own_send(1, j, to_y).start()
        own_send(3, j, to_pair).start()
    for copy in id_copies:
        copy.wait()
    expert_rows = lax.broadcasted_iota(jnp.int32, (table.shape[1], group), 0)
    share = jnp.zeros((table.shape[1], group), jnp.float32)
    for k in range(ids_v.shape[0]):
        share = share + jnp.where(ids_v[k : k + 1, :] == expert_rows, wts_v[k : k + 1, :], 0.0)
    same = lax.broadcasted_iota(jnp.int32, (group, group), 0) == lax.broadcasted_iota(jnp.int32, (group, group), 1)
    table[rows_of(own), :] = lax.dot_general(
        same.astype(jnp.float32), share, (((1,), (1,)), ((), ())),
        precision=lax.Precision.HIGHEST, preferred_element_type=jnp.float32,
    )
    table_copies = [
        remote(table.at[rows_of(own), :], table.at[rows_of(own), :], t_send.at[p], t_recv.at[p], target)
        for p, target in plane
    ]
    for copy in table_copies:
        copy.start()
    for j in range(chunks):
        weight_copy(2, j).start()

    own_copy.wait()

    def relay_step(s, carry):
        forward(0, g_x, s, to_x).wait_recv()

        @pl.when(s % 2 == 0)
        def _():
            diagonal(s).start()

        forward(4, g_x, s, to_pair).start()
        forward(1, g_y, s, to_y).wait_recv()

        @pl.when(s % 2 == 1)
        def _():
            diagonal(s).start()

        forward(5, g_y, s, to_pair).start()
        return carry

    def gather_step(s, carry):
        @pl.when(s < chunks)
        def _():
            forward(2, g_d, s, to_y).wait_recv()
            forward(6, g_d, s, to_pair).start()

        @pl.when(s >= 1)
        def _():
            j = s - 1
            for kind, g in enumerate(pair_groups):
                forward(3 + kind, g, j, to_pair).wait_recv()
            weight_copy(0, j).wait()
            weight_copy(1, j).wait()
            lhs = rows_all[:, cols_of(j)]
            gate_acc[...] += row_product(lhs, wg_v[:, cols_of(j)])
            up_acc[...] += row_product(lhs, wu_v[:, cols_of(j)])

        return carry

    lax.fori_loop(0, chunks, relay_step, 0)
    lax.fori_loop(0, chunks + 1, gather_step, 0)
    act[...] = (jax.nn.silu(gate_acc[...]) * up_acc[...]).astype(act.dtype)

    for p, _ in plane:
        source = number((y + dp_count - p // expert_count) % dp_count,
                        (e + expert_count - p % expert_count) % expert_count)
        remote(table.at[rows_of(source), :], table.at[rows_of(source), :],
               t_send.at[p], t_recv.at[p], to_pair).wait_recv()
    lane_all = lax.broadcasted_iota(jnp.int32, table.shape, 1)
    coef = jnp.sum(
        jnp.where(lane_all == e * tensor_count + z, table[...], 0.0), axis=1, keepdims=True
    )
    for j in range(chunks):
        weight_copy(2, j).wait()

    a, b = x + c * (y - x), y + c * (x - y)
    to_a = device(y + c * (1 - 2 * y), e + (1 - c) * (xe - e), z)
    to_b = device(y + (1 - c) * (1 - 2 * y), e + c * (xe - e), z)

    def block_rows(s, u):
        return pl.ds(pl.multiple_of((s * (1 + c) + u * (2 - c)) * block, block), block)

    steps = [(i, r) for r in range(len(rounds)) for i in range(tensor_count)]

    def span(k):
        i, r = steps[k]
        return slice(i * quarter + rounds[r][0], i * quarter + rounds[r][0] + rounds[r][1])

    def place(h, q, r):
        return pl.ds(pl.multiple_of(h * half + q * quarter + rounds[r][0], 128), rounds[r][1])

    def pair_copy(k):
        return remote(pair_send.at[:, span(k)], pair_recv.at[:, span(k)], pa_send.at[k], pa_recv.at[k], to_pair)

    def a_copy(k):
        return remote(a_send.at[:, :, span(k)], a_recv.at[:, :, span(k)], aa_send.at[k], aa_recv.at[k], to_a)

    def b_copy(k):
        return remote(b_send.at[:, span(k)], b_recv.at[:, span(k)], ba_send.at[k], ba_recv.at[k], to_b)

    def c_copy(k):
        i, r = steps[k]
        return remote(c_send.at[:, span(k)], c_recv.at[:, span(k)], ca_send.at[k], ca_recv.at[k],
                      device(y, e, (z + 1 + i) % tensor_count))

    def f_copy(d, o, r, target):
        rows = rows_of(c if o == 0 else 1 - c)
        place_r = slice(rounds[r][0], rounds[r][0] + rounds[r][1])
        n = (r * tensor_count + d) * 2 + o
        return remote(f_send.at[rows, place_r], gathered.at[:, place(c, z, r)], fa_send.at[n], fa_recv.at[n], target)

    def compute(k):
        i, r = steps[k]
        q = (z + 1 + i) % tensor_count
        away = jnp.dot(act[...], wd_v[:, place(1 - c, q, r)], preferred_element_type=jnp.float32)
        pair_send[:, span(k)] = (away * coef).astype(pair_send.dtype)
        pair_copy(k).start()
        kept = jnp.dot(act[...], wd_v[:, place(c, q, r)], preferred_element_type=jnp.float32)
        part[:, span(k)] = kept * coef

    def both(s, u, k):
        rows = block_rows(s, u)
        return part[rows, span(k)] + pair_recv[rows, span(k)].astype(jnp.float32)

    def stage_a(k):
        pair_copy(k).wait_recv()
        for u in range(2):
            a_send[u, :, span(k)] = both(1 - a, u, k).astype(a_send.dtype)
        a_copy(k).start()

    def stage_b(k):
        a_copy(k).wait_recv()
        total = both(a, 1 - b, k) + a_recv[1 - b, :, span(k)].astype(jnp.float32)
        b_send[:, span(k)] = total.astype(b_send.dtype)
        b_copy(k).start()

    def stage_c(k):
        i, r = steps[k]
        b_copy(k).wait_recv()
        total = both(a, b, k) + a_recv[b, :, span(k)].astype(jnp.float32)
        total = total + b_recv[:, span(k)].astype(jnp.float32)
        if i < tensor_count - 1:
            c_send[:, span(k)] = total.astype(c_send.dtype)
            c_copy(k).start()
            return
        own_total[:, rounds[r][0] : rounds[r][0] + rounds[r][1]] = total

    def stage_f(r):
        place_r = slice(rounds[r][0], rounds[r][0] + rounds[r][1])
        total = own_total[:, place_r]
        for other in range(tensor_count - 1):
            n = r * tensor_count + other
            c_copy(n).wait_recv()
            total = total + c_recv[:, span(n)].astype(jnp.float32)
        f_send[:, place_r] = total.astype(f_send.dtype)
        for d, o, target in reversed(line[1:]):
            f_copy(d, o, r, target).start()
        gathered[:, place(c, z, r)] = f_send[rows_of(c), place_r]

    for t in range(len(steps) + lags[3]):
        for lag, stage in zip((0,) + lags[:3], (compute, stage_a, stage_b, stage_c)):
            if 0 <= t - lag < len(steps):
                stage(t - lag)
        if t >= lags[3] and steps[t - lags[3]][0] == tensor_count - 1:
            stage_f(steps[t - lags[3]][1])

    def f_arrival(d, o, r):
        source_z = (z + tensor_count - d) % tensor_count
        n = (r * tensor_count + d) * 2 + o
        spot = gathered.at[:, place(c if o == 0 else 1 - c, source_z, r)]
        return remote(spot, spot, fa_send.at[n], fa_recv.at[n], to_pair)

    def gather_sent(j, carry):
        own_send(0, j, to_x).wait_send()
        own_send(1, j, to_y).wait_send()
        own_send(3, j, to_pair).wait_send()
        diagonal(j).wait_send()
        forward(4, g_x, j, to_pair).wait_send()
        forward(5, g_y, j, to_pair).wait_send()
        forward(6, g_d, j, to_pair).wait_send()
        return carry

    lax.fori_loop(0, chunks, gather_sent, 0)
    for copy in table_copies:
        copy.wait_send()
    for k in range(len(steps)):
        pair_copy(k).wait_send()
        a_copy(k).wait_send()
        b_copy(k).wait_send()
        if steps[k][0] < tensor_count - 1:
            c_copy(k).wait_send()
    for r in range(len(rounds)):
        for d, o, target in line[1:]:
            f_arrival(d, o, r).wait_recv()
            f_copy(d, o, r, target).wait_send()
    out[...] = gathered[...]


def fused_body(shape, hidden_rows, expert_ids, route_weights, w_gate, w_up, w_down):
    dp_count, expert_count, tensor_count = shape["dp"], shape["expert"], shape["tensor"]
    group, width = hidden_rows.shape
    hidden = w_gate.shape[1]
    rows = dp_count * expert_count * group
    half = width // 2
    quarter = half // tensor_count
    chunks = split_count(width, 256, 8)
    rounds = ((0, quarter),)
    count = len(rounds) * tensor_count
    lanes = -(-expert_count * tensor_count // 128) * 128
    dma = pltpu.SemaphoreType.DMA
    bf16, f32 = jnp.bfloat16, jnp.float32
    any_space = pl.BlockSpec(memory_space=pl.ANY)
    vmem_space = pl.BlockSpec(memory_space=pltpu.VMEM)
    scratch = [
        pltpu.VMEM((rows, width), bf16),
        pltpu.VMEM((hidden, width), bf16),
        pltpu.VMEM((hidden, width), bf16),
        pltpu.VMEM((hidden, width), bf16),
        pltpu.VMEM((rows, hidden), f32),
        pltpu.VMEM((rows, hidden), f32),
        pltpu.VMEM((rows, hidden), bf16),
        pltpu.VMEM((rows, lanes), f32),
        pltpu.VMEM((rows, half), bf16),
        pltpu.VMEM((rows, half), bf16),
        pltpu.VMEM((rows, half), f32),
        pltpu.VMEM((2, 2 * group, half), bf16),
        pltpu.VMEM((2, 2 * group, half), bf16),
        pltpu.VMEM((2 * group, half), bf16),
        pltpu.VMEM((2 * group, half), bf16),
        pltpu.VMEM((2 * group, half), bf16),
        pltpu.VMEM((2 * group, half), bf16),
        pltpu.VMEM((2 * group, quarter), bf16),
        pltpu.VMEM((2 * group, quarter), f32),
        pltpu.VMEM((group, width), bf16),
        pltpu.VMEM(expert_ids.shape[::-1], expert_ids.dtype),
        pltpu.VMEM(route_weights.shape[::-1], route_weights.dtype),
        dma,
        dma((2,)),
        dma((3, chunks)),
        dma((7, chunks)), dma((7, chunks)),
        dma((dp_count * expert_count,)), dma((dp_count * expert_count,)),
        dma((count,)), dma((count,)),
        dma((count,)), dma((count,)),
        dma((count,)), dma((count,)),
        dma((count,)), dma((count,)),
        dma((2 * count,)), dma((2 * count,)),
    ]
    return pl.pallas_call(
        functools.partial(fused_kernel, (dp_count, expert_count, tensor_count, chunks), rounds, (1, 4, 6, 7)),
        out_shape=jax.ShapeDtypeStruct((group, width), bf16),
        in_specs=[any_space] * 6,
        out_specs=vmem_space,
        scratch_shapes=scratch,
        compiler_params=pltpu.CompilerParams(
            collective_id=0, has_side_effects=True, vmem_limit_bytes=60 * 1024 * 1024
        ),
        name="routed_experts",
    )(hidden_rows, expert_ids.T, route_weights.T, w_gate, w_up, w_down)


def body(shape, hidden_rows, expert_ids, route_weights, w_gate, w_up, w_down):
    dp_count, expert_count, tensor_count = shape["dp"], shape["expert"], shape["tensor"]
    group, width = hidden_rows.shape
    chosen = expert_ids.shape[1]
    dense = 2 * group * chosen >= group * expert_count * tensor_count
    square = dp_count == 2 and expert_count == 2 * dp_count
    aligned = width % (256 * tensor_count) == 0 and group % 16 == 0
    chosen_body = general_body
    if dense and square and aligned and tensor_count > 1 and w_gate.shape[0] == 1:
        chosen_body = functools.partial(fused_body, shape)
    return chosen_body(hidden_rows, expert_ids, route_weights, w_gate, w_up, w_down)


def solution(mesh):
    return jax.shard_map(
        functools.partial(body, dict(mesh.shape)),
        mesh=mesh,
        in_specs=(
            P(("dp", "expert"), None),
            P(("dp", "expert"), None),
            P(("dp", "expert"), None),
            P(("expert", "tensor"), "dp", None),
            P(("expert", "tensor"), "dp", None),
            P(("expert", "tensor"), "dp", None),
        ),
        out_specs=P(("dp", "expert"), None),
        check_vma=False,
    )
```

profile of v0, /device:TPU:0, one launch (start us, length us, event | category | flops | bytes accessed | tf_op | source)
XLA Modules:
  0.0 47.5 jit_solution(17694486033055967516)
XLA Ops:
  0.0 45.9 %routed_experts.1 = bf16[16,7168]{1,0:T(8,128)(2,1)} custom-call(bf16[16,7168]{1,0:T(8,128)(2,1)} %hid.1, s32[8,16]{1,0:T(8,128)} %bitcast.2, f32[8,16]{1,0:T(8,128)} %bitcast.3, bf16[1,512,7168]{2,1,0:T(8,128)(2,1)} %wg.1, bf16[1,512,7168]{2,1,0:T(8,128)(2,1)} %wu.1, bf16[1,512,7168]{2,1,0:T(8,128)(2,1)} %wd.1), custom_call_target="tpu_custom_call" | custom-call | tf_op jit(solution)/shard_map/routed_experts/pallas_call | solution.py:430
  45.9 1.6 %copy.8 = bf16[16,7168]{1,0:T(8,128)(2,1)} copy(bf16[16,7168]{1,0:T(8,128)(2,1)} %routed_experts.1) | data formatting | bytes 458752
where the time goes:
time: 47.7 us; the launch traced here: 47.5 us
  Pallas kernels  45.9 us (96%)
  local copies, waits for them, and re-layouts  1.64 us (3%)
    pallas_call x1, Pallas kernels, fused_body(): pl.pallas_call(functools.partial(fused_kernel, (dp_count, expert_count, t...  45.9 us
    unnamed x1, local copies, waits for them, and re-layouts  1.64 us

commit v1 on v0

--- a/solution.py
+++ b/solution.py
@@ -90,14 +90,15 @@
 
 
 def fused_kernel(
-    sizes, rounds, lags,
+    sizes, rounds, plan,
     hid, ids, wts, wg, wu, wd, out,
     rows_all, wg_v, wu_v, wd_v, gate_acc, up_acc, act, table,
-    pair_send, pair_recv, part, a_send, a_recv, b_send, b_recv, c_send, c_recv, f_send, own_total, gathered,
-    ids_v, wts_v, own_sem, id_sem, w_sem, g_send, g_recv, t_send, t_recv, pa_send, pa_recv, aa_send, aa_recv,
-    ba_send, ba_recv, ca_send, ca_recv, fa_send, fa_recv,
+    pair_send, pair_recv, part, a_send, a_recv, b_send, b_recv, c_send, c_recv, f_send, own_total,
+    ids_v, wts_v, own_sem, id_sem, w_sem, wd_sem, g_recv, sent_sem, t_recv, pa_recv, aa_recv, ba_recv, ca_recv,
+    fa_recv, o_sem,
 ):
     dp_count, expert_count, tensor_count, chunks = sizes
+    depth, gather_times, return_times = plan
     group, width = hid.shape
     chunk = width // chunks
     half = width // 2
@@ -118,13 +119,25 @@
         return pl.ds(pl.multiple_of(g * group, group), group)
 
     def cols_of(j):
-        return pl.ds(pl.multiple_of(j * chunk, chunk), chunk)
+        return slice(j * chunk, (j + 1) * chunk)
 
     def remote(src, dst, send, recv, target):
         return pltpu.make_async_remote_copy(
             src_ref=src, dst_ref=dst, send_sem=send, recv_sem=recv,
             device_id=target, device_id_type=pl.DeviceIdType.MESH,
         )
+
+    def in_order(table):
+        return sorted((start + step * k, n, k) for n, (count, start, step) in enumerate(table) for k in range(count))
+
+    own = number(y, e)
+    own_copy = pltpu.make_async_copy(hid, rows_all.at[rows_of(own), :], own_sem)
+    own_copy.start()
+    id_copies = [
+        pltpu.make_async_copy(ids, ids_v, id_sem.at[0]), pltpu.make_async_copy(wts, wts_v, id_sem.at[1])
+    ]
+    for copy in id_copies:
+        copy.start()
 
     plane = [
         (p, device((y + p // expert_count) % dp_count, (e + p % expert_count) % expert_count, z))
@@ -139,121 +152,103 @@
     for target in greeted:
         pl.semaphore_signal(barrier, inc=1, device_id=target, device_id_type=pl.DeviceIdType.MESH)
 
-    own = number(y, e)
-    own_copy = pltpu.make_async_copy(hid, rows_all.at[rows_of(own), :], own_sem)
-    own_copy.start()
-    id_copies = [
-        pltpu.make_async_copy(ids, ids_v, id_sem.at[0]), pltpu.make_async_copy(wts, wts_v, id_sem.at[1])
-    ]
-    for copy in id_copies:
-        copy.start()
-
     def weight_copy(which, j):
         src, dst = ((wg, wg_v), (wu, wu_v), (wd, wd_v))[which]
-        return pltpu.make_async_copy(src.at[0, :, cols_of(j)], dst.at[:, cols_of(j)], w_sem.at[which, j])
-
+        sem = wd_sem if which == 2 else w_sem.at[j]
+        return pltpu.make_async_copy(src.at[0, :, cols_of(j)], dst.at[:, cols_of(j)], sem)
+
+    to_x, to_y, to_pair = device(y, xe, z), device(yy, e, z), device(y, ce, z)
+    g_x, g_y, g_d = number(y, xe), number(yy, e), number(yy, xe)
+    g_sent, t_sent, p_sent, a_sent, b_sent, c_sent, f_sent = (sent_sem.at[n] for n in range(7))
+
+    def piece(g, j):
+        return rows_all.at[rows_of(g), cols_of(j)]
+
+    def forward(kind, g, j, target):
+        return remote(piece(g, j), piece(g, j), g_sent, g_recv.at[min(kind, 3), j], target)
+
+    def own_send(kind, j):
+        return remote(piece(own, j), piece(own, j), g_sent, g_recv.at[kind, j], (to_x, to_y, None, to_pair)[kind])
+
+    def diagonal(j):
+        return forward(2, g_x, j, to_y) if j % 2 == 0 else forward(2, g_y, j, to_x)
+
+    own_copy.wait()
+    pl.semaphore_wait(barrier, len(greeted))
+    for j in range(depth):
+        for kind in (0, 1, 3):
+            own_send(kind, j).start()
     for j in range(chunks):
         weight_copy(0, j).start()
         weight_copy(1, j).start()
-    gate_acc[...] = jnp.zeros_like(gate_acc)
-    up_acc[...] = jnp.zeros_like(up_acc)
-    pl.semaphore_wait(barrier, len(greeted))
-
-    to_x, to_y, to_pair = device(y, xe, z), device(yy, e, z), device(y, ce, z)
-    g_x, g_y, g_d = number(y, xe), number(yy, e), number(yy, xe)
-    pair_groups = (number(y, ce), number(y, cxe), number(yy, ce), number(yy, cxe))
-
-    def piece(g, j):
-        return rows_all.at[rows_of(g), cols_of(j)]
-
-    def own_send(kind, j, target):
-        return remote(hid.at[:, cols_of(j)], piece(own, j), g_send.at[kind, j], g_recv.at[kind, j], target)
-
-    def forward(kind, g, j, target):
-        return remote(piece(g, j), piece(g, j), g_send.at[kind, j], g_recv.at[kind, j], target)
-
-    def diagonal(j):
-        odd = j % 2
-        target = device(y + (1 - odd) * (1 - 2 * y), e + odd * (xe - e), z)
-        return forward(2, g_x + odd * (g_y - g_x), j, target)
-
-    for j in range(chunks):
-        own_send(0, j, to_x).start()
-        own_send(1, j, to_y).start()
-        own_send(3, j, to_pair).start()
-    for copy in id_copies:
-        copy.wait()
-    expert_rows = lax.broadcasted_iota(jnp.int32, (table.shape[1], group), 0)
-    share = jnp.zeros((table.shape[1], group), jnp.float32)
-    for k in range(ids_v.shape[0]):
-        share = share + jnp.where(ids_v[k : k + 1, :] == expert_rows, wts_v[k : k + 1, :], 0.0)
-    same = lax.broadcasted_iota(jnp.int32, (group, group), 0) == lax.broadcasted_iota(jnp.int32, (group, group), 1)
-    table[rows_of(own), :] = lax.dot_general(
-        same.astype(jnp.float32), share, (((1,), (1,)), ((), ())),
-        precision=lax.Precision.HIGHEST, preferred_element_type=jnp.float32,
-    )
-    table_copies = [
-        remote(table.at[rows_of(own), :], table.at[rows_of(own), :], t_send.at[p], t_recv.at[p], target)
-        for p, target in plane
-    ]
-    for copy in table_copies:
-        copy.start()
     for j in range(chunks):
         weight_copy(2, j).start()
 
-    own_copy.wait()
-
-    def relay_step(s, carry):
+    table_copies = [
+        remote(table.at[rows_of(own), :], table.at[rows_of(own), :], t_sent, t_recv, target) for _, target in plane
+    ]
+
+    def share_table(_):
+        for copy in id_copies:
+            copy.wait()
+        expert_rows = lax.broadcasted_iota(jnp.int32, (table.shape[1], group), 0)
+        share = jnp.zeros((table.shape[1], group), jnp.float32)
+        for k in range(ids_v.shape[0]):
+            share = share + jnp.where(ids_v[k : k + 1, :] == expert_rows, wts_v[k : k + 1, :], 0.0)
+        same = lax.broadcasted_iota(jnp.int32, (group, group), 0) == lax.broadcasted_iota(jnp.int32, (group, group), 1)
+        table[rows_of(own), :] = lax.dot_general(
+            same.astype(jnp.float32), share, (((1,), (1,)), ((), ())),
+            precision=lax.Precision.HIGHEST, preferred_element_type=jnp.float32,
+        )
+        for copy in table_copies:
+            copy.start()
+
+    def relay(s):
+        later = s + depth < chunks
         forward(0, g_x, s, to_x).wait_recv()
-
-        @pl.when(s % 2 == 0)
-        def _():
+        if s % 2 == 0:
             diagonal(s).start()
-
+        if later:
+            own_send(1, s + depth).start()
         forward(4, g_x, s, to_pair).start()
         forward(1, g_y, s, to_y).wait_recv()
-
-        @pl.when(s % 2 == 1)
-        def _():
+        if s % 2 == 1:
             diagonal(s).start()
-
+        if later:
+            own_send(0, s + depth).start()
+            own_send(3, s + depth).start()
         forward(5, g_y, s, to_pair).start()
-        return carry
-
-    def gather_step(s, carry):
-        @pl.when(s < chunks)
-        def _():
-            forward(2, g_d, s, to_y).wait_recv()
-            forward(6, g_d, s, to_pair).start()
-
-        @pl.when(s >= 1)
-        def _():
-            j = s - 1
-            for kind, g in enumerate(pair_groups):
-                forward(3 + kind, g, j, to_pair).wait_recv()
-            weight_copy(0, j).wait()
-            weight_copy(1, j).wait()
-            lhs = rows_all[:, cols_of(j)]
-            gate_acc[...] += row_product(lhs, wg_v[:, cols_of(j)])
-            up_acc[...] += row_product(lhs, wu_v[:, cols_of(j)])
-
-        return carry
-
-    lax.fori_loop(0, chunks, relay_step, 0)
-    lax.fori_loop(0, chunks + 1, gather_step, 0)
+
+    def relay_far(s):
+        forward(2, g_d, s, to_y).wait_recv()
+        forward(6, g_d, s, to_pair).start()
+
+    def project(acc, weight, j):
+        value = row_product(rows_all[:, cols_of(j)], weight[:, cols_of(j)])
+        acc[...] = value if j == 0 else acc[...] + value
+
+    def gate(j):
+        arrived = rows_all.at[0 : rows_all.shape[0] // 2, cols_of(j)]
+        remote(arrived, arrived, g_sent, g_recv.at[3, j], to_pair).wait_recv()
+        filled = wg_v.at[:, 0 : 2 * chunk]
+        pltpu.make_async_copy(filled, filled, w_sem.at[j]).wait()
+        project(gate_acc, wg_v, j)
+
+    def up(j):
+        project(up_acc, wu_v, j)
+
+    gather_stages = (relay, relay_far, gate, up, share_table)
+    for _, n, k in in_order(gather_times):
+        gather_stages[n](k)
     act[...] = (jax.nn.silu(gate_acc[...]) * up_acc[...]).astype(act.dtype)
 
-    for p, _ in plane:
-        source = number((y + dp_count - p // expert_count) % dp_count,
-                        (e + expert_count - p % expert_count) % expert_count)
-        remote(table.at[rows_of(source), :], table.at[rows_of(source), :],
-               t_send.at[p], t_recv.at[p], to_pair).wait_recv()
+    others = table.at[0 : len(plane) * group, :]
+    remote(others, others, t_sent, t_recv, to_pair).wait_recv()
     lane_all = lax.broadcasted_iota(jnp.int32, table.shape, 1)
     coef = jnp.sum(
         jnp.where(lane_all == e * tensor_count + z, table[...], 0.0), axis=1, keepdims=True
     )
-    for j in range(chunks):
-        weight_copy(2, j).wait()
+    pltpu.make_async_copy(wd_v, wd_v, wd_sem).wait()
 
     a, b = x + c * (y - x), y + c * (x - y)
     to_a = device(y + c * (1 - 2 * y), e + (1 - c) * (xe - e), z)
@@ -272,24 +267,23 @@
         return pl.ds(pl.multiple_of(h * half + q * quarter + rounds[r][0], 128), rounds[r][1])
 
     def pair_copy(k):
-        return remote(pair_send.at[:, span(k)], pair_recv.at[:, span(k)], pa_send.at[k], pa_recv.at[k], to_pair)
+        return remote(pair_send.at[:, span(k)], pair_recv.at[:, span(k)], p_sent, pa_recv.at[k], to_pair)
 
     def a_copy(k):
-        return remote(a_send.at[:, :, span(k)], a_recv.at[:, :, span(k)], aa_send.at[k], aa_recv.at[k], to_a)
+        return remote(a_send.at[:, :, span(k)], a_recv.at[:, :, span(k)], a_sent, aa_recv.at[k], to_a)
 
     def b_copy(k):
-        return remote(b_send.at[:, span(k)], b_recv.at[:, span(k)], ba_send.at[k], ba_recv.at[k], to_b)
+        return remote(b_send.at[:, span(k)], b_recv.at[:, span(k)], b_sent, ba_recv.at[k], to_b)
 
     def c_copy(k):
         i, r = steps[k]
-        return remote(c_send.at[:, span(k)], c_recv.at[:, span(k)], ca_send.at[k], ca_recv.at[k],
+        return remote(c_send.at[:, span(k)], c_recv.at[:, span(k)], c_sent, ca_recv.at[r],
                       device(y, e, (z + 1 + i) % tensor_count))
 
-    def f_copy(d, o, r, target):
+    def f_copy(o, r, target):
         rows = rows_of(c if o == 0 else 1 - c)
         place_r = slice(rounds[r][0], rounds[r][0] + rounds[r][1])
-        n = (r * tensor_count + d) * 2 + o
-        return remote(f_send.at[rows, place_r], gathered.at[:, place(c, z, r)], fa_send.at[n], fa_recv.at[n], target)
+        return remote(f_send.at[rows, place_r], out.at[:, place(c, z, r)], f_sent, fa_recv, target)
 
     def compute(k):
         i, r = steps[k]
@@ -328,54 +322,36 @@
         own_total[:, rounds[r][0] : rounds[r][0] + rounds[r][1]] = total
 
     def stage_f(r):
-        place_r = slice(rounds[r][0], rounds[r][0] + rounds[r][1])
+        low, size = rounds[r]
+        place_r = slice(low, low + size)
+        filled = c_recv.at[:, 0 : (tensor_count - 1) * size]
+        remote(filled, filled, c_sent, ca_recv.at[r], to_pair).wait_recv()
         total = own_total[:, place_r]
         for other in range(tensor_count - 1):
-            n = r * tensor_count + other
-            c_copy(n).wait_recv()
-            total = total + c_recv[:, span(n)].astype(jnp.float32)
+            total = total + c_recv[:, span(r * tensor_count + other)].astype(jnp.float32)
         f_send[:, place_r] = total.astype(f_send.dtype)
-        for d, o, target in reversed(line[1:]):
-            f_copy(d, o, r, target).start()
-        gathered[:, place(c, z, r)] = f_send[rows_of(c), place_r]
-
-    for t in range(len(steps) + lags[3]):
-        for lag, stage in zip((0,) + lags[:3], (compute, stage_a, stage_b, stage_c)):
-            if 0 <= t - lag < len(steps):
-                stage(t - lag)
-        if t >= lags[3] and steps[t - lags[3]][0] == tensor_count - 1:
-            stage_f(steps[t - lags[3]][1])
-
-    def f_arrival(d, o, r):
-        source_z = (z + tensor_count - d) % tensor_count
-        n = (r * tensor_count + d) * 2 + o
-        spot = gathered.at[:, place(c if o == 0 else 1 - c, source_z, r)]
-        return remote(spot, spot, fa_send.at[n], fa_recv.at[n], to_pair)
-
-    def gather_sent(j, carry):
-        own_send(0, j, to_x).wait_send()
-        own_send(1, j, to_y).wait_send()
-        own_send(3, j, to_pair).wait_send()
-        diagonal(j).wait_send()
-        forward(4, g_x, j, to_pair).wait_send()
-        forward(5, g_y, j, to_pair).wait_send()
-        forward(6, g_d, j, to_pair).wait_send()
-        return carry
-
-    lax.fori_loop(0, chunks, gather_sent, 0)
-    for copy in table_copies:
-        copy.wait_send()
-    for k in range(len(steps)):
-        pair_copy(k).wait_send()
-        a_copy(k).wait_send()
-        b_copy(k).wait_send()
-        if steps[k][0] < tensor_count - 1:
-            c_copy(k).wait_send()
-    for r in range(len(rounds)):
-        for d, o, target in line[1:]:
-            f_arrival(d, o, r).wait_recv()
-            f_copy(d, o, r, target).wait_send()
-    out[...] = gathered[...]
+        for _, o, target in reversed(line[1:]):
+            f_copy(o, r, target).start()
+        pltpu.make_async_copy(f_send.at[rows_of(c), place_r], out.at[:, place(c, z, r)], o_sem).start()
+
+    return_stages = (compute, stage_a, stage_b, stage_c, stage_f)
+    for _, n, k in in_order(return_times):
+        return_stages[n](k)
+
+    def sent(ref, sem):
+        remote(ref, ref, sem, t_recv, to_pair).wait_send()
+
+    sent(rows_all.at[0 : 7 * group, :], g_sent)
+    sent(others, t_sent)
+    sent(pair_send, p_sent)
+    sent(a_send, a_sent)
+    sent(b_send, b_sent)
+    sent(c_send.at[:, 0 : (tensor_count - 1) * quarter], c_sent)
+    from_others = out.at[:, 0 : width - quarter]
+    sent(from_others, f_sent)
+    remote(from_others, from_others, f_sent, fa_recv, to_pair).wait_recv()
+    kept_rows = out.at[:, 0:quarter]
+    pltpu.make_async_copy(kept_rows, kept_rows, o_sem).wait()
 
 
 def fused_body(shape, hidden_rows, expert_ids, route_weights, w_gate, w_up, w_down):
@@ -385,14 +361,19 @@
     rows = dp_count * expert_count * group
     half = width // 2
     quarter = half // tensor_count
-    chunks = split_count(width, 256, 8)
-    rounds = ((0, quarter),)
+    chunks = split_count(width, 256, 7)
+    rounds = split_rounds(quarter, 1)
     count = len(rounds) * tensor_count
     lanes = -(-expert_count * tensor_count // 128) * 128
+    gather_times = (
+        (chunks, 2.4, 0.85), (chunks, 5.1, 0.8), (chunks, 6.1, 0.8), (chunks, 6.45, 0.8), (1, 7.55, 0.0),
+    )
+    return_times = (
+        (count, 0.0, 0.62), (count, 1.6, 0.62), (count, 5.0, 1.6), (count, 8.6, 1.4), (len(rounds), 15.0, 5.0),
+    )
     dma = pltpu.SemaphoreType.DMA
     bf16, f32 = jnp.bfloat16, jnp.float32
     any_space = pl.BlockSpec(memory_space=pl.ANY)
-    vmem_space = pl.BlockSpec(memory_space=pltpu.VMEM)
     scratch = [
         pltpu.VMEM((rows, width), bf16),
         pltpu.VMEM((hidden, width), bf16),
@@ -413,25 +394,30 @@
         pltpu.VMEM((2 * group, half), bf16),
         pltpu.VMEM((2 * group, quarter), bf16),
         pltpu.VMEM((2 * group, quarter), f32),
-        pltpu.VMEM((group, width), bf16),
         pltpu.VMEM(expert_ids.shape[::-1], expert_ids.dtype),
         pltpu.VMEM(route_weights.shape[::-1], route_weights.dtype),
         dma,
         dma((2,)),
-        dma((3, chunks)),
-        dma((7, chunks)), dma((7, chunks)),
-        dma((dp_count * expert_count,)), dma((dp_count * expert_count,)),
-        dma((count,)), dma((count,)),
-        dma((count,)), dma((count,)),
-        dma((count,)), dma((count,)),
-        dma((count,)), dma((count,)),
-        dma((2 * count,)), dma((2 * count,)),
+        dma((chunks,)),
+        dma,
+        dma((4, chunks)),
+        dma((7,)),
+        dma,
+        dma((count,)),
+        dma((count,)),
+        dma((count,)),
+        dma((len(rounds),)),
+        dma,
+        dma,
     ]
     return pl.pallas_call(
-        functools.partial(fused_kernel, (dp_count, expert_count, tensor_count, chunks), rounds, (1, 4, 6, 7)),
+        functools.partial(
+            fused_kernel, (dp_count, expert_count, tensor_count, chunks), rounds,
+            (4, gather_times, return_times),
+        ),
         out_shape=jax.ShapeDtypeStruct((group, width), bf16),
         in_specs=[any_space] * 6,
-        out_specs=vmem_space,
+        out_specs=any_space,
         scratch_shapes=scratch,
         compiler_params=pltpu.CompilerParams(
             collective_id=0, has_side_effects=True, vmem_limit_bytes=60 * 1024 * 1024

time: 47.7 us -> 43.8 us (0.918)
  Pallas kernels: 45.9 us -> 42 us
    pallas_call x1, Pallas kernels: 45.9 us -> 42 us  [fused_body(): pl.pallas_call(functools.partial(fused_kernel, (dp_count, expert_count, t...]
where the time goes in v1:
time: 43.8 us; the launch traced here: 43.6 us
  Pallas kernels  42 us (96%)
  local copies, waits for them, and re-layouts  1.64 us (4%)
    pallas_call x1, Pallas kernels, fused_body(): pl.pallas_call(functools.partial(fused_kernel, (dp_count, expert_count, t...  42 us
    unnamed x1, local copies, waits for them, and re-layouts  1.64 us

profile of v1, /device:TPU:0, one launch (start us, length us, event | category | flops | bytes accessed | tf_op | source)
XLA Modules:
  0.0 43.6 jit_solution(8936587435918230296)
XLA Ops:
  0.0 42.0 %routed_experts.1 = bf16[16,7168]{1,0:T(8,128)(2,1)} custom-call(bf16[16,7168]{1,0:T(8,128)(2,1)} %hid.1, s32[8,16]{1,0:T(8,128)} %bitcast.2, f32[8,16]{1,0:T(8,128)} %bitcast.3, bf16[1,512,7168]{2,1,0:T(8,128)(2,1)} %wg.1, bf16[1,512,7168]{2,1,0:T(8,128)(2,1)} %wu.1, bf16[1,512,7168]{2,1,0:T(8,128)(2,1)} %wd.1), custom_call_target="tpu_custom_call" | custom-call | tf_op jit(solution)/shard_map/routed_experts/pallas_call | solution.py:413
  42.0 1.6 %copy.8 = bf16[16,7168]{1,0:T(8,128)(2,1)} copy(bf16[16,7168]{1,0:T(8,128)(2,1)} %routed_experts.1) | data formatting | bytes 458752

commit v2 on v1

--- a/solution.py
+++ b/solution.py
@@ -200,6 +200,8 @@
             same.astype(jnp.float32), share, (((1,), (1,)), ((), ())),
             precision=lax.Precision.HIGHEST, preferred_element_type=jnp.float32,
         )
+
+    def send_table(_):
         for copy in table_copies:
             copy.start()
 
@@ -237,7 +239,7 @@
     def up(j):
         project(up_acc, wu_v, j)
 
-    gather_stages = (relay, relay_far, gate, up, share_table)
+    gather_stages = (relay, relay_far, gate, up, send_table, share_table)
     for _, n, k in in_order(gather_times):
         gather_stages[n](k)
     act[...] = (jax.nn.silu(gate_acc[...]) * up_acc[...]).astype(act.dtype)
@@ -362,14 +364,15 @@
     half = width // 2
     quarter = half // tensor_count
     chunks = split_count(width, 256, 7)
-    rounds = split_rounds(quarter, 1)
+    rounds = split_rounds(quarter, 2)
     count = len(rounds) * tensor_count
     lanes = -(-expert_count * tensor_count // 128) * 128
     gather_times = (
         (chunks, 2.4, 0.85), (chunks, 5.1, 0.8), (chunks, 6.1, 0.8), (chunks, 6.45, 0.8), (1, 7.55, 0.0),
+        (1, 7.54, 0.0),
     )
     return_times = (
-        (count, 0.0, 0.62), (count, 1.6, 0.62), (count, 5.0, 1.6), (count, 8.6, 1.4), (len(rounds), 15.0, 5.0),
+        (count, 0, 0.32), (count, 1.0, 0.4), (count, 4.4, 0.8), (count, 7.2, 0.9), (len(rounds), 13.0, 3.0),
     )
     dma = pltpu.SemaphoreType.DMA
     bf16, f32 = jnp.bfloat16, jnp.float32
@@ -415,9 +418,9 @@
             fused_kernel, (dp_count, expert_count, tensor_count, chunks), rounds,
             (4, gather_times, return_times),
         ),
-        out_shape=jax.ShapeDtypeStruct((group, width), bf16),
+        out_shape=pltpu.VMEM((group, width), bf16),
         in_specs=[any_space] * 6,
-        out_specs=any_space,
+        out_specs=pl.BlockSpec(memory_space=pltpu.VMEM),
         scratch_shapes=scratch,
         compiler_params=pltpu.CompilerParams(
             collective_id=0, has_side_effects=True, vmem_limit_bytes=60 * 1024 * 1024

time: 43.8 us -> 42.3 us (0.966)
  local copies, waits for them, and re-layouts: 1.64 us -> 0.69 us
  Pallas kernels: 42 us -> 41.5 us
    unnamed x1, local copies, waits for them, and re-layouts: 1.64 us -> 0.69 us
    pallas_call x1, Pallas kernels: 42 us -> 41.5 us  [fused_body(): pl.pallas_call(functools.partial(fused_kernel, (dp_count, expert_count, t...]
where the time goes in v2:
time: 42.3 us; the launch traced here: 42.2 us
  Pallas kernels  41.5 us (98%)
  local copies, waits for them, and re-layouts  0.69 us (2%)
    pallas_call x1, Pallas kernels, fused_body(): pl.pallas_call(functools.partial(fused_kernel, (dp_count, expert_count, t...  41.5 us

profile of v2, /device:TPU:0, one launch (start us, length us, event | category | flops | bytes accessed | tf_op | source)
XLA Modules:
  0.0 42.2 jit_solution(7221482079932658862)
XLA Ops:
  0.0 41.5 %routed_experts.1 = bf16[16,7168]{1,0:T(8,128)(2,1)S(1)} custom-call(bf16[16,7168]{1,0:T(8,128)(2,1)} %hid.1, s32[8,16]{1,0:T(8,128)} %bitcast.2, f32[8,16]{1,0:T(8,128)} %bitcast.3, bf16[1,512,7168]{2,1,0:T(8,128)(2,1)} %wg.1, bf16[1,512,7168]{2,1,0:T(8,128)(2,1)} %wu.1, bf16[1,512,7168]{2,1,0:T(8,128)(2,1)} %wd.1), custom_call_target="tpu_custom_call" | custom-call | tf_op jit(solution)/shard_map/routed_experts/pallas_call | solution.py:416
  41.5 0.7 %copy.8 = bf16[16,7168]{1,0:T(8,128)(2,1)} copy(bf16[16,7168]{1,0:T(8,128)(2,1)S(1)} %routed_experts.1) | data formatting | bytes 458752
